TPU v7x, 32 devices: a whole 2x2x4 slice. The times are simulated.
32 devices in a mesh: dp: 16 (over z, x, core), tensor: 2 (over y).
Axes of the slice: x: 2, y: 2, z: 4, core: 2. Of those that a mesh axis runs over, the one named last changes fastest.
Arguments:
- inputs: bfloat16 [640, 64, 1024], P('tensor', 'dp'), may hold values from -6 to 6
- pad_mask: int32 [64, 640], P('dp'), may hold values from 0 to 1, as said below
- norm1_gain: bfloat16 [2, 512], P('tensor', 'dp'), may hold values from 0.099609375 to 1.8984375
- norm1_shift: bfloat16 [2, 512], P('tensor', 'dp'), may hold values from -3 to 3
- qkv_weight: bfloat16 [1024, 3, 1024], P('dp', None, 'tensor'), may hold values from -0.1875 to 0.1875
- qv_bias: bfloat16 [2, 2, 512], P(None, 'tensor', 'dp'), may hold values from -3 to 3
- out_weight: bfloat16 [1024, 1024], P('tensor', 'dp'), may hold values from -3 to 3
- out_bias: bfloat16 [2, 512], P('tensor', 'dp'), may hold values from -3 to 3
- norm2_gain: bfloat16 [2, 512], P('tensor', 'dp'), may hold values from 0.099609375 to 1.8984375
- norm2_shift: bfloat16 [2, 512], P('tensor', 'dp'), may hold values from -3 to 3
- up_weight: bfloat16 [1024, 4096], P('dp', 'tensor'), may hold values from -0.1875 to 0.1875
- up_bias: bfloat16 [2, 2048], P('tensor', 'dp'), may hold values from -3 to 3
- down_weight: bfloat16 [4096, 1024], P('tensor', 'dp'), may hold values from -0.09375 to 0.09375
- down_bias: bfloat16 [2, 512], P('tensor', 'dp'), may hold values from -3 to 3
- cotangent: float32 [640, 64, 1024], P('tensor', 'dp'), may hold values from -6 to 6
Outputs:
- block_output: float32 [640, 64, 1024], P('tensor', 'dp')
- input_grad: float32 [640, 64, 1024], P('tensor', 'dp')
- gain_one_grad: float32 [2, 512], P('tensor', 'dp')
- shift_one_grad: float32 [2, 512], P('tensor', 'dp')
- qkv_weight_grad: float32 [1024, 3, 1024], P('dp', None, 'tensor')
- qv_bias_grad: float32 [2, 2, 512], P(None, 'tensor', 'dp')
- out_weight_grad: float32 [1024, 1024], P('tensor', 'dp')
- out_bias_grad: float32 [2, 512], P('tensor', 'dp')
- gain_two_grad: float32 [2, 512], P('tensor', 'dp')
- shift_two_grad: float32 [2, 512], P('tensor', 'dp')
- up_weight_grad: float32 [1024, 4096], P('dp', 'tensor')
- up_bias_grad: float32 [2, 2048], P('tensor', 'dp')
- down_weight_grad: float32 [4096, 1024], P('tensor', 'dp')
- down_bias_grad: float32 [2, 512], P('tensor', 'dp')
Inputs may be any that keep to these rules, and one draw needn't show every extreme that they name: `pad_mask`: each image's row holds ones on its first slots and zeros after them; it has between 289 and 577 ones, and image 0 has exactly 577.
All inputs are finite; a program needn't handle non-finite values.
Results may differ from a plain program's by a relative error of at most 0.0085.
The roundings to bfloat16 on the way count: a program that leaves them out, or rounds other values in their place, can miss the bound.
Values may be sent and summed in bfloat16 or wider, within the bound.
No kernel may reach another device: no remote copies, remote signals or barrier semaphores. Data moves between devices by JAX's collectives and lax.ppermute only.
A program may use at most 256 MiB of HBM per device.

v0:
```python
import jax
import jax.numpy as jnp
from jax import lax
from jax.sharding import PartitionSpec as P

HD = 64
epsilon = 1e-06
masked_score = -1e30


def layer_norm(values, gain, shift):
    row_mean = jnp.mean(values, axis=-1, keepdims=True)
    centred = values - row_mean
    spread = jnp.mean(centred * centred, axis=-1, keepdims=True)
    return centred * lax.rsqrt(spread + epsilon) * gain + shift


def gelu_exact(values):
    return jax.nn.gelu(values, approximate=False)


def image_scores(queries, key_rows, kept_row):
    scores = jnp.einsum(
        "qhe,khe->hqk", queries, key_rows, preferred_element_type=jnp.float32
    ) * HD ** (-0.5)
    return jnp.where(kept_row[None, None, :], scores, masked_score)


def forward_image(operands):
    queries, key_rows, value_rows, kept_row = operands
    scores = image_scores(queries, key_rows, kept_row)
    row_max = jnp.max(scores, axis=-1, keepdims=True)
    exps = jnp.exp(scores - row_max)
    row_total = jnp.sum(exps, axis=-1, keepdims=True)
    soft_weights = (exps / row_total).astype(jnp.bfloat16)
    attended = jnp.einsum(
        "hqk,khe->qhe", soft_weights, value_rows, preferred_element_type=jnp.float32
    )
    return (attended.astype(jnp.bfloat16), (row_max + jnp.log(row_total))[..., 0])


def backward_image(operands):
    queries, key_rows, value_rows, kept_row, log_total, attended_grad = operands
    seq_length = queries.shape[0]
    scores = image_scores(queries, key_rows, kept_row)
    soft_float = jnp.exp(scores - log_total[..., None])
    soft_weights = soft_float.astype(jnp.bfloat16)
    value_grad = jnp.einsum(
        "hqk,qhe->khe", soft_weights, attended_grad, preferred_element_type=jnp.float32
    )
    prob_grad = jnp.einsum(
        "qhe,khe->hqk", attended_grad, value_rows, preferred_element_type=jnp.float32
    )
    score_grad = soft_float * (prob_grad - jnp.sum(prob_grad * soft_float, axis=-1, keepdims=True))
    score_grad = score_grad.astype(jnp.bfloat16)
    query_grad = jnp.einsum(
        "hqk,khe->qhe", score_grad, key_rows, preferred_element_type=jnp.float32
    ) * HD ** (-0.5)
    key_grad = jnp.einsum(
        "hqk,qhe->khe", score_grad, queries, preferred_element_type=jnp.float32
    ) * HD ** (-0.5)
    joined = jnp.concatenate(
        [
            query_grad.reshape(seq_length, -1),
            key_grad.reshape(seq_length, -1),
            value_grad.reshape(seq_length, -1),
        ],
        axis=-1,
    )
    return joined.astype(jnp.bfloat16)


def on_device(
    inputs,
    pad_mask,
    norm1_gain,
    norm1_shift,
    qkv_weight,
    qv_bias,
    out_weight,
    out_bias,
    norm2_gain,
    norm2_shift,
    up_weight,
    up_bias,
    down_weight,
    down_bias,
    cotangent,
):
    local_rows = inputs.shape[0]
    image_count = inputs.shape[1]
    model_width = inputs.shape[2]
    seq_length = pad_mask.shape[1]
    tensor_count = lax.axis_size("tensor")
    vector_stack = jnp.stack(
        [norm1_gain, norm1_shift, out_bias, norm2_gain, norm2_shift, down_bias], axis=0
    )
    gathered = (
        lax.all_gather(qkv_weight, "dp", axis=0, tiled=True),
        lax.all_gather(out_weight, "dp", axis=1, tiled=True),
        lax.all_gather(up_weight, "dp", axis=0, tiled=True),
        lax.all_gather(down_weight, "dp", axis=1, tiled=True),
        lax.all_gather(qv_bias, "dp", axis=2, tiled=True),
        lax.all_gather(up_bias, "dp", axis=1, tiled=True),
        lax.all_gather(vector_stack, "dp", axis=2, tiled=True),
    )
    qkv_full, out_full, up_full, down_full, bias_pair, bias_hidden, vector_part = gathered
    local_width = qkv_full.shape[2]
    head_count = local_width // HD
    vector_rows = (
        lax.all_gather(vector_part, "tensor", axis=1, tiled=True)
        .reshape(6, model_width)
        .astype(jnp.float32)
    )
    gain_one, shift_one, out_shift, gain_two, shift_two, down_shift = [
        vector_rows[index] for index in range(6)
    ]
    qkv_matrix = qkv_full.reshape(model_width, 3 * local_width)
    bias_row = jnp.concatenate(
        [
            bias_pair[0, 0].astype(jnp.float32),
            jnp.zeros((local_width,), jnp.float32),
            bias_pair[1, 0].astype(jnp.float32),
        ]
    )
    up_row = bias_hidden.reshape(-1).astype(jnp.float32)
    kept_all = pad_mask > 0
    first_row = lax.axis_index("tensor") * local_rows
    kept_float = jnp.transpose(lax.dynamic_slice_in_dim(kept_all, first_row, local_rows, 1)).astype(
        jnp.float32
    )[:, :, None]
    input_float = inputs.astype(jnp.float32)
    normed_one = layer_norm(input_float, gain_one, shift_one).astype(jnp.bfloat16)
    normed_all = lax.all_gather(normed_one, "tensor", axis=0, tiled=True)
    qkv_rows = (
        jnp.einsum("sbd,dc->sbc", normed_all, qkv_matrix, preferred_element_type=jnp.float32)
        + bias_row
    )
    qkv_rows = qkv_rows.astype(jnp.bfloat16)
    qkv_images = jnp.swapaxes(qkv_rows, 0, 1).reshape(image_count, seq_length, 3, head_count, HD)
    query_all = qkv_images[:, :, 0]
    key_all = qkv_images[:, :, 1]
    value_all = qkv_images[:, :, 2]
    attended_img, log_totals = lax.map(forward_image, (query_all, key_all, value_all, kept_all))
    attended_rows = jnp.swapaxes(attended_img.reshape(image_count, seq_length, local_width), 0, 1)
    row_block = attended_rows
    projected = lax.psum_scatter(
        jnp.einsum("sbc,cd->sbd", row_block, out_full, preferred_element_type=jnp.float32),
        "tensor",
        scatter_dimension=0,
        tiled=True,
    )
    after_attn = input_float + projected + out_shift
    normed_two = layer_norm(after_attn, gain_two, shift_two).astype(jnp.bfloat16)
    normed_all_two = lax.all_gather(normed_two, "tensor", axis=0, tiled=True)
    up_values = (
        jnp.einsum("sbd,df->sbf", normed_all_two, up_full, preferred_element_type=jnp.float32)
        + up_row
    )
    activated = gelu_exact(up_values).astype(jnp.bfloat16)
    row_block = activated
    mlp_out = lax.psum_scatter(
        jnp.einsum("sbf,fd->sbd", row_block, down_full, preferred_element_type=jnp.float32),
        "tensor",
        scatter_dimension=0,
        tiled=True,
    )
    block_output = (after_attn + mlp_out + down_shift) * kept_float
    qkv_back, out_back, up_back, down_back = (qkv_matrix, out_full, up_full, down_full)
    out_grad = cotangent * kept_float
    down_shift_grad = jnp.sum(out_grad, axis=(0, 1))
    out_low = out_grad.astype(jnp.bfloat16)
    out_low_all = lax.all_gather(out_low, "tensor", axis=0, tiled=True)
    down_weight_grad = jnp.einsum(
        "sbf,sbd->fd", activated, out_low_all, preferred_element_type=jnp.float32
    )
    act_grad = jnp.einsum("sbd,fd->sbf", out_low_all, down_back, preferred_element_type=jnp.float32)
    _, gelu_back = jax.vjp(gelu_exact, up_values)
    up_grad = gelu_back(act_grad)[0].astype(jnp.bfloat16)
    up_shift_grad = jnp.sum(up_grad.astype(jnp.float32), axis=(0, 1))
    up_weight_grad = jnp.einsum(
        "sbd,sbf->df", normed_all_two, up_grad, preferred_element_type=jnp.float32
    )
    row_block = up_grad
    normed_two_grad = lax.psum_scatter(
        jnp.einsum("sbf,df->sbd", row_block, up_back, preferred_element_type=jnp.float32),
        "tensor",
        scatter_dimension=0,
        tiled=True,
    )
    _, norm_two_back = jax.vjp(layer_norm, after_attn, gain_two, shift_two)
    attn_side, gain_two_grad, shift_two_grad = norm_two_back(normed_two_grad)
    after_attn_grad = out_grad + attn_side
    out_shift_grad = jnp.sum(after_attn_grad, axis=(0, 1))
    proj_low = after_attn_grad.astype(jnp.bfloat16)
    proj_low_all = lax.all_gather(proj_low, "tensor", axis=0, tiled=True)
    out_weight_grad = jnp.einsum(
        "sbc,sbd->cd", attended_rows, proj_low_all, preferred_element_type=jnp.float32
    )
    attended_grad = jnp.einsum(
        "sbd,cd->sbc", proj_low_all, out_back, preferred_element_type=jnp.float32
    )
    attended_grad = attended_grad.astype(jnp.bfloat16)
    attended_grad_img = jnp.swapaxes(attended_grad, 0, 1).reshape(
        image_count, seq_length, head_count, HD
    )
    qkv_grad_img = lax.map(
        backward_image, (query_all, key_all, value_all, kept_all, log_totals, attended_grad_img)
    )
    qkv_grad = jnp.swapaxes(qkv_grad_img, 0, 1)
    qkv_sums = jnp.sum(qkv_grad.astype(jnp.float32), axis=(0, 1))
    qv_grad = jnp.stack([qkv_sums[:local_width], qkv_sums[2 * local_width :]], axis=0).reshape(
        2, 1, local_width
    )
    qkv_weight_grad = jnp.einsum(
        "sbd,sbc->dc", normed_all, qkv_grad, preferred_element_type=jnp.float32
    )
    qkv_weight_grad = qkv_weight_grad.reshape(model_width, 3, local_width)
    row_block = qkv_grad
    normed_one_grad = lax.psum_scatter(
        jnp.einsum("sbc,dc->sbd", row_block, qkv_back, preferred_element_type=jnp.float32),
        "tensor",
        scatter_dimension=0,
        tiled=True,
    )
    _, norm_one_back = jax.vjp(layer_norm, input_float, gain_one, shift_one)
    input_side, gain_one_grad, shift_one_grad = norm_one_back(normed_one_grad)
    input_grad = after_attn_grad + input_side
    vector_grads = jnp.stack(
        [
            gain_one_grad,
            shift_one_grad,
            out_shift_grad,
            gain_two_grad,
            shift_two_grad,
            down_shift_grad,
        ],
        axis=0,
    ).reshape(6, tensor_count, model_width // tensor_count)
    vector_local = lax.psum_scatter(vector_grads, "tensor", scatter_dimension=1, tiled=True)
    owned = (
        lax.psum_scatter(qkv_weight_grad, "dp", scatter_dimension=0, tiled=True),
        lax.psum_scatter(out_weight_grad, "dp", scatter_dimension=1, tiled=True),
        lax.psum_scatter(up_weight_grad, "dp", scatter_dimension=0, tiled=True),
        lax.psum_scatter(down_weight_grad, "dp", scatter_dimension=1, tiled=True),
        lax.psum_scatter(qv_grad, "dp", scatter_dimension=2, tiled=True),
        lax.psum_scatter(up_shift_grad.reshape(1, -1), "dp", scatter_dimension=1, tiled=True),
        lax.psum_scatter(vector_local, "dp", scatter_dimension=2, tiled=True),
    )
    qkv_owned, out_owned, up_owned, down_owned, qv_owned, hidden_owned, vector_owned = owned
    return (
        block_output,
        input_grad,
        vector_owned[0],
        vector_owned[1],
        qkv_owned,
        qv_owned,
        out_owned,
        vector_owned[2],
        vector_owned[3],
        vector_owned[4],
        up_owned,
        hidden_owned,
        down_owned,
        vector_owned[5],
    )


def solution(mesh):
    in_specs = (
        P("tensor", "dp", None),
        P("dp", None),
        P("tensor", "dp"),
        P("tensor", "dp"),
        P("dp", None, "tensor"),
        P(None, "tensor", "dp"),
        P("tensor", "dp"),
        P("tensor", "dp"),
        P("tensor", "dp"),
        P("tensor", "dp"),
        P("dp", "tensor"),
        P("tensor", "dp"),
        P("tensor", "dp"),
        P("tensor", "dp"),
        P("tensor", "dp", None),
    )
    out_specs = (
        P("tensor", "dp", None),
        P("tensor", "dp", None),
        P("tensor", "dp"),
        P("tensor", "dp"),
        P("dp", None, "tensor"),
        P(None, "tensor", "dp"),
        P("tensor", "dp"),
        P("tensor", "dp"),
        P("tensor", "dp"),
        P("tensor", "dp"),
        P("dp", "tensor"),
        P("tensor", "dp"),
        P("tensor", "dp"),
        P("tensor", "dp"),
    )
    return jax.shard_map(
        on_device, mesh=mesh, in_specs=in_specs, out_specs=out_specs, check_vma=False
    )
```

profile of v0, /device:TPU:0, one launch (start us, length us, event | category | flops | bytes accessed | tf_op | source)
XLA Modules:
  0.0 1860.6 jit_solution(15390352596484088534)
XLA Ops:
  12.1 23.8 %all_gather.36 = bf16[6,1,512]{0,1,2:T(2,128)(2,1)S(1)} all-gather(bf16[6,1,32]{0,1,2:T(2,128)(2,1)S(1)} %copy.88), channel_id=1, replica_groups=mesh['dp'=16,'tensor'=2] {'dp'}, dimensions={2}, use_global_device_ids=true | all-gather | bytes 6528 | tf_op jit(solution)/shard_map/all_gather | solution.py:105
  49.8 18.0 all_gather.40
  73.5 54.6 %all-gather.9.cloned.1.call-done = bf16[640,4,1024]{2,0,1:T(8,128)(2,1)} async-done(((bf16[320,4,1024]{2,0,1:T(8,128)(2,1)}), bf16[640,4,1024]{2,0,1:T(8,128)(2,1)}) %all-gather.9.cloned.1.call-update) | async-done | bytes 5242896 | tf_op jit(solution)/shard_map/all_gather | solution.py:134
  128.1 12.9 fusion.50
  141.0 10.6 copy.93
  157.0 51.5 %while.22 = (s32[]{:T(128)}, bf16[4,640,8,64]{1,3,2,0:T(8,128)(2,1)}, f32[4,8,640]{2,1,0:T(8,128)}, bf16[4,640,8,64]{1,3,2,0:T(8,128)(2,1)}, pred[4,640]{1,0:T(4...) while((s32[]{:T(128)}, ...), condition=%wide.region_5.6_spmd, body=%wide.region_2.5_spmd.sunk | while | flops 878504960 | bytes 42113112 | solution.py:144
  213.5 8.9 fusion.80
  223.5 120.9 %reduce-scatter.18.cloned.1.call-done = f32[320,4,1024]{2,0,1:T(8,128)} async-done(((f32[640,4,1024]{2,0,1:T(8,128)}), f32[320,4,1024]{2,0,1:T(8,128)}) %reduce-scatter.18.cloned.1.call-update) | async-done | bytes 5242896 | tf_op jit(solution)/shard_map/reduce_scatter | solution.py:147
  353.2 7.3 fusion.77
  361.3 21.3 %all_gather.44 = bf16[1,2048]{1,0:T(2,128)(2,1)S(1)} all-gather(bf16[1,128]{1,0:T(2,128)(2,1)S(1)} %copy-done.29), channel_id=1, replica_groups=mesh['dp'=16,'tensor'=2] {'dp'}, dimensions={1}, use_global_device_ids=true | all-gather | bytes 4352 | tf_op jit(solution)/shard_map/all_gather | solution.py:104
  382.7 14.3 all-gather.17.cloned.1.call-done
  397.0 68.5 %all-gather.15.cloned.1.call-done = bf16[640,4,1024]{2,0,1:T(8,128)(2,1)} async-done(((bf16[320,4,1024]{2,0,1:T(8,128)(2,1)}), bf16[640,4,1024]{2,0,1:T(8,128)(2,1)}) %all-gather.15.cloned.1.call-update) | async-done | bytes 5242896 | tf_op jit(solution)/shard_map/all_gather | solution.py:155
  465.5 24.9 %fusion.68 = (u8[640,2048]{1,0:T(8,128)(4,1)S(1)}, u8[640,2048]{1,0:T(8,128)(4,1)S(1)}, f32[640,4,2048]{2,0,1:T(8,128)}) fusion(f32[2048]{0:T(1024)S(1)} %bitcast.227, bf16[640,4,1024]{2,0,1:T(8,128)(2,1)} %all-gather.15.cloned.1.call-done, bf16[1024,2048]{1,0:T(8,128)(2,1)} %all-gather.17.cloned.1.call-done), kind=kOutput, calls=%fused_computation.110 | convolution fusion | flops 10808197120 | bytes 33038336 | tf_op jit(solution)/shard_map/sbd,df->sbf/dot_general | solution.py:157
  490.4 51.1 %multiply_convert_fusion.1 = (bf16[640,4,2048]{2,0,1:T(8,128)(2,1)}, f32[640,4,2048]{2,0,1:T(8,128)}) fusion(f32[640,4,2048]{2,0,1:T(8,128)} %get-tuple-element.224, f32[2048]{0:T(1024)S(1)} %bitcast.228, u8[640,2048]{1,0:T(8,128)(4,1)S(1)} %get-tuple-element.154, u8[640,2048]{1,0:T(8,128)(4,1)S(1)} %get-tuple-element.153), kind=kLoop, calls=%fused_computation.64 | loop fusion | flops 372244480 | bytes 55058432 | tf_op jit(solution)/shard_map/convert_element_type | solution.py:160
  541.5 46.9 %all-gather.19.cloned.1.call-done = bf16[2048,1024]{0,1:T(8,128)(2,1)} async-done(((bf16[2048,64]{0,1:T(8,128)(2,1)}), bf16[2048,1024]{0,1:T(8,128)(2,1)}) %all-gather.19.cloned.1.call-update) | async-done | bytes 4194320 | tf_op jit(solution)/shard_map/all_gather | solution.py:102
  588.4 27.9 %convert_reduce_fusion = (f32[2048]{0:T(1024)}, bf16[640,4,2048]{2,0,1:T(8,128)(2,1)}) fusion(f32[640,4,2048]{2,0,1:T(8,128)} %get-tuple-element.198, bf16[640,4,1024]{2,0,1:T(8,128)(2,1)} %all-gather.21.cloned.1.call-done, bf16[2048,1024]{0,1:T(8,128)(2,1)} %all-gather.19.cloned.1.call-done, f32[640,4,2048]{2,0,1:T(8,128)} %get-tuple-element.224, ...), kind=kOutput, calls=%fused_computation.62 | convolution fusion | flops 10826545152 | bytes 61882368 | tf_op jit(solution)/shard_map/sbd,fd->sbf/dot_general | solution.py:177
  616.3 17.4 fusion.72
  633.8 17.5 fusion.70
  651.4 102.8 %reduce-scatter.22.cloned.1.call-done = f32[320,4,1024]{2,0,1:T(8,128)} async-done(((f32[640,4,1024]{2,0,1:T(8,128)}), f32[320,4,1024]{2,0,1:T(8,128)}) %reduce-scatter.22.cloned.1.call-update) | async-done | bytes 5242896 | tf_op jit(solution)/shard_map/reduce_scatter | solution.py:185
  754.2 6.0 fusion.93
  765.0 113.3 %reduce-scatter.20.cloned.1.call-done = f32[320,4,1024]{2,0,1:T(8,128)} async-done(((f32[640,4,1024]{2,0,1:T(8,128)}), f32[320,4,1024]{2,0,1:T(8,128)}) %reduce-scatter.20.cloned.1.call-update) | async-done | bytes 5242896 | tf_op jit(solution)/shard_map/reduce_scatter | solution.py:162
  878.3 11.7 fusion.95
  894.7 68.3 %all-gather.23.cloned.1.call-done = bf16[640,4,1024]{2,0,1:T(8,128)(2,1)} async-done(((bf16[320,4,1024]{2,0,1:T(8,128)(2,1)}), bf16[640,4,1024]{2,0,1:T(8,128)(2,1)}) %all-gather.23.cloned.1.call-update) | async-done | bytes 5242896 | tf_op jit(solution)/shard_map/all_gather | solution.py:196
  962.9 7.2 convolution_convert_fusion
  970.2 113.1 %while.23 = (s32[]{:T(128)}, bf16[4,640,1536]{1,2,0:T(8,128)(2,1)}, bf16[4,640,8,64]{1,3,2,0:T(8,128)(2,1)S(1)}, pred[4,640]{1,0:T(4,128)(4,1)S(1)}, bf16[4,640,...) while((s32[]{:T(128)}, bf16[4,640,1536]{1,2,0:T(8,128)(2,1)}, ...), condition=%wide.region_15.16_spmd, body=%wide.region_13.15_spmd.sunk | while | flops 2134174720 | bytes 108898144 | solution.py:207
  975.4 7.9 multiply_reduce_fusion.5
  983.3 5.9 multiply_convert_fusion.3
  1003.7 7.9 multiply_reduce_fusion.5
  1011.6 5.9 multiply_convert_fusion.3
  1032.0 7.9 multiply_reduce_fusion.5
  1039.8 5.9 multiply_convert_fusion.3
  1060.3 7.9 multiply_reduce_fusion.5
  1068.1 5.9 multiply_convert_fusion.3
  1083.3 14.2 fusion.53
  1105.6 13.3 fusion.51
  1118.9 9.6 copy.100
  1129.8 89.7 %reduce-scatter.24.cloned.1.call-done = f32[320,4,1024]{2,0,1:T(8,128)} async-done(((f32[640,4,1024]{2,0,1:T(8,128)}), f32[320,4,1024]{2,0,1:T(8,128)}) %reduce-scatter.24.cloned.1.call-update) | async-done | bytes 5242896 | tf_op jit(solution)/shard_map/reduce_scatter | solution.py:220
  1227.6 7.3 all-reduce
  1240.5 17.4 convolution_bitcast_fusion.1
  1258.0 17.5 convolution_bitcast_fusion
  1275.8 7.6 fusion.83
  1286.1 8.2 copy.101
  1294.4 44.9 %reduce-scatter.34.cloned.1.call-done = f32[32,2]{1,0:T(8,128)} async-done(((f32[512,2]{1,0:T(8,128)}), f32[32,2]{1,0:T(8,128)}) %reduce-scatter.34.cloned.1.call-update) | async-done | bytes 272
  1340.7 171.6 %all-reduce.4.cloned.1.call-done = f32[1024,3,512]{2,1,0:T(4,128)} async-done(((f32[1024,3,512]{2,1,0:T(4,128)}), f32[1024,3,512]{2,1,0:T(4,128)}) %all-reduce.4.cloned.1.call-update) | async-done | bytes 6291472
  1525.3 45.6 %reduce-scatter.32.cloned.1.call-done = f32[32,6]{1,0:T(8,128)} async-done(((f32[512,6]{1,0:T(8,128)}), f32[32,6]{1,0:T(8,128)}) %reduce-scatter.32.cloned.1.call-update) | async-done | bytes 784
  1575.3 103.8 %reduce-scatter.28.cloned.1.call-done = f32[64,2048]{1,0:T(8,128)} async-done(((f32[1024,2048]{1,0:T(8,128)}), f32[64,2048]{1,0:T(8,128)}) %reduce-scatter.28.cloned.1.call-update) | async-done | bytes 524304 | tf_op jit(solution)/shard_map/reduce_scatter | solution.py:244
  1679.0 108.9 %reduce-scatter.30.cloned.1.call-done = f32[2048,64]{0,1:T(8,128)} async-done(((f32[2048,1024]{0,1:T(8,128)}), f32[2048,64]{0,1:T(8,128)}) %reduce-scatter.30.cloned.1.call-update) | async-done | bytes 524304 | tf_op jit(solution)/shard_map/reduce_scatter | solution.py:245
  1788.0 65.7 %reduce-scatter.26.cloned.1.call-done = f32[512,64]{0,1:T(8,128)} async-done(((f32[512,1024]{0,1:T(8,128)}), f32[512,64]{0,1:T(8,128)}) %reduce-scatter.26.cloned.1.call-update) | async-done | bytes 131088 | tf_op jit(solution)/shard_map/reduce_scatter | solution.py:243
  (234 shorter events, 208.2 us)
Async XLA Ops:
  7.2 36.4 %copy-start.1 = (bf16[320,4,1024]{2,1,0:T(4,128)(2,1)S(1)}, bf16[320,4,1024]{2,1,0:T(4,128)(2,1)}, u32[]{:S(2)}) copy-start(bf16[320,4,1024]{2,1,0:T(4,128)(2,1)} %param.19) | copy-start | bytes 7864324
  7.2 63.0 %all-gather.11.cloned.1.call-start = ((), (), s32[]{:S(2)}) async-start(), calls=%async_computation.11 | async-start | bytes 3342336 | tf_op jit(solution)/shard_map/all_gather | solution.py:99
  7.9 120.2 %all-gather.9.cloned.1.call-start = ((), (), s32[]{:S(2)}) async-start(), calls=%async_computation.10 | async-start | bytes 7864320 | tf_op jit(solution)/shard_map/all_gather | solution.py:134
  43.6 2.2 copy-start.10
  43.6 6.1 copy-start.28
  43.6 26.5 %copy-start.26 = (s32[4,640]{1,0:T(4,128)S(1)}, s32[4,640]{1,0:T(4,128)}, u32[]{:S(2)}) copy-start(s32[4,640]{1,0:T(4,128)} %param.20) | copy-start | bytes 30724
  48.9 164.6 %all-gather.13.cloned.1.call-start = ((), (), s32[]{:S(2)}) async-start(), calls=%async_computation.12 | async-start | bytes 1114112 | tf_op jit(solution)/shard_map/all_gather | solution.py:100
  49.6 294.8 %reduce-scatter.18.cloned.1.call-start = ((), (), s32[]{:S(2)}) async-start(), calls=%async_computation.13 | async-start | bytes 15728640 | tf_op jit(solution)/shard_map/reduce_scatter | solution.py:147
  73.5 67.5 %copy-start.9 = (bf16[1024,3,512]{0,2,1:T(8,128)(2,1)}, bf16[1024,3,512]{0,2,1:T(8,128)(2,1)S(1)}, u32[]{:S(2)}) copy-start(bf16[1024,3,512]{0,2,1:T(8,128)(2,1)S(1)} %copy.90) | copy-start | bytes 9437188
  208.6 13.9 copy-start.7
  222.4 122.0 %copy-start.2 = (bf16[320,4,1024]{2,1,0:T(4,128)(2,1)S(1)}, bf16[320,4,1024]{2,1,0:T(4,128)(2,1)}, u32[]{:S(2)}) copy-start(bf16[320,4,1024]{2,1,0:T(4,128)(2,1)} %param.19) | copy-start | bytes 7864324
  222.4 122.0 %copy-start.22 = (f32[1,2,512]{2,0,1:T(1,128)S(1)}, f32[1,2,512]{2,0,1:T(1,128)}, u32[]{:S(2)}) copy-start(f32[1,2,512]{2,0,1:T(1,128)} %get-tuple-element.219) | copy-start | bytes 12292
  222.4 174.6 %all-gather.17.cloned.1.call-start = ((), (), s32[]{:S(2)}) async-start(), calls=%async_computation.15 | async-start | bytes 4456448 | tf_op jit(solution)/shard_map/all_gather | solution.py:101
  223.0 242.5 %all-gather.15.cloned.1.call-start = ((), (), s32[]{:S(2)}) async-start(), calls=%async_computation.14 | async-start | bytes 7864320 | tf_op jit(solution)/shard_map/all_gather | solution.py:155
  348.6 2.4 copy-start
  348.6 2.4 copy-start.12
  348.6 2.3 copy-start.19
  353.0 188.5 %all-gather.21.cloned.1.call-start = ((), (), s32[]{:S(2)}) async-start(), calls=%async_computation.18 | async-start | bytes 7864320 | tf_op jit(solution)/shard_map/all_gather | solution.py:173
  353.2 8.2 copy-start.29
  360.5 227.9 %all-gather.19.cloned.1.call-start = ((), (), s32[]{:S(2)}) async-start(), calls=%async_computation.16 | async-start | bytes 4456448 | tf_op jit(solution)/shard_map/all_gather | solution.py:102
  361.3 392.9 %reduce-scatter.22.cloned.1.call-start = ((), (), s32[]{:S(2)}) async-start(), calls=%async_computation.19 | async-start | bytes 15728640 | tf_op jit(solution)/shard_map/reduce_scatter | solution.py:185
  633.7 244.5 %reduce-scatter.20.cloned.1.call-start = ((), (), s32[]{:S(2)}) async-start(), calls=%async_computation.17 | async-start | bytes 15728640 | tf_op jit(solution)/shard_map/reduce_scatter | solution.py:162
  651.3 311.6 %all-gather.23.cloned.1.call-start = ((), (), s32[]{:S(2)}) async-start(), calls=%async_computation.20 | async-start | bytes 7864320 | tf_op jit(solution)/shard_map/all_gather | solution.py:196
  754.2 6.0 copy-start.4
  760.2 118.1 %copy-start.21 = (f32[1,2,512]{2,0,1:T(1,128)S(1)}, f32[1,2,512]{2,0,1:T(1,128)}, u32[]{:S(2)}) copy-start(f32[1,2,512]{2,0,1:T(1,128)} %get-tuple-element.216) | copy-start | bytes 12292
  889.9 2.3 copy-start.6
  894.2 325.3 %reduce-scatter.24.cloned.1.call-start = ((), (), s32[]{:S(2)}) async-start(), calls=%async_computation.21 | async-start | bytes 15728640 | tf_op jit(solution)/shard_map/reduce_scatter | solution.py:220
  894.7 75.5 %copy-start.8 = (bf16[4,640,8,64]{1,3,2,0:T(8,128)(2,1)S(1)}, bf16[4,640,8,64]{1,3,2,0:T(8,128)(2,1)}, u32[]{:S(2)}) copy-start(bf16[4,640,8,64]{1,3,2,0:T(8,128)(2,1)} %copy-done.7) | copy-start | bytes 7864324
  1097.5 0.7 copy-start.27
  1097.5 187.2 %reduce-scatter.36.cloned.1.call-start = ((), (), s32[]{:S(2)}) async-start(), calls=%async_computation.27 | async-start | bytes 1114112
  1099.5 239.7 %reduce-scatter.34.cloned.1.call-start = ((), (), s32[]{:S(2)}) async-start(), calls=%async_computation.26 | async-start | bytes 278528
  1105.6 406.7 %all-reduce.4.cloned.1.call-start = ((), (), s32[]{:S(2)}) async-start(), calls=%async_computation.28 | async-start | bytes 16777216
  1128.5 0.7 copy-start.31
  1128.5 1.2 copy-start.25
  1128.5 1.2 copy-start.20
  1128.5 1.3 copy-start.23
  1128.5 1.3 copy-start.24
  1128.5 91.0 %copy-start.3 = (bf16[320,4,1024]{2,1,0:T(4,128)(2,1)S(1)}, bf16[320,4,1024]{2,1,0:T(4,128)(2,1)}, u32[]{:S(2)}) copy-start(bf16[320,4,1024]{2,1,0:T(4,128)(2,1)} %param.19) | copy-start | bytes 7864324
  1128.5 91.0 %copy-start.11 = (f32[320,4]{0,1:T(4,128)S(1)}, f32[320,4]{0,1:T(4,128)}, u32[]{:S(2)}) copy-start(f32[320,4]{0,1:T(4,128)} %copy-done.10) | copy-start | bytes 15364
  1128.5 91.0 %copy-start.14 = (f32[1,2,512]{2,0,1:T(1,128)S(1)}, f32[1,2,512]{2,0,1:T(1,128)}, u32[]{:S(2)}) copy-start(f32[1,2,512]{2,0,1:T(1,128)} %copy-done.13) | copy-start | bytes 12292
  1128.6 95.3 %copy-start.18 = (f32[320,4]{0,1:T(4,128)S(1)}, f32[320,4]{0,1:T(4,128)}, u32[]{:S(2)}) copy-start(f32[320,4]{0,1:T(4,128)} %copy-done.17) | copy-start | bytes 15364
  1128.6 95.4 %copy-start.16 = (f32[320,4]{0,1:T(4,128)S(1)}, f32[320,4]{0,1:T(4,128)}, u32[]{:S(2)}) copy-start(f32[320,4]{0,1:T(4,128)} %copy-done.15) | copy-start | bytes 15364
  1128.6 442.3 %reduce-scatter.32.cloned.1.call-start = ((), (), s32[]{:S(2)}) async-start(), calls=%async_computation.25 | async-start | bytes 278528
  1219.5 4.5 copy-start.5
  1240.5 438.5 %reduce-scatter.28.cloned.1.call-start = ((), (), s32[]{:S(2)}) async-start(), calls=%async_computation.23 | async-start | bytes 8912896 | tf_op jit(solution)/shard_map/reduce_scatter | solution.py:244
  1258.0 530.0 %reduce-scatter.30.cloned.1.call-start = ((), (), s32[]{:S(2)}) async-start(), calls=%async_computation.24 | async-start | bytes 8912896 | tf_op jit(solution)/shard_map/reduce_scatter | solution.py:245
  1275.5 8.0 copy-start.30
  1275.5 578.1 %reduce-scatter.26.cloned.1.call-start = ((), (), s32[]{:S(2)}) async-start(), calls=%async_computation.22 | async-start | bytes 2228224 | tf_op jit(solution)/shard_map/reduce_scatter | solution.py:243
  (3 other events, 1.9 us)
Sparse Core Ops, SparseCore 0:
  10.2 48.9 all-gather.10
  60.8 67.2 all-gather.8
  130.3 37.9 all-gather.12
  222.6 121.7 reduce-scatter.17
  346.4 50.5 all-gather.16
  398.4 67.0 all-gather.14
  467.1 68.5 all-gather.20
  537.8 50.5 all-gather.18
  633.8 120.3 reduce-scatter.21
  756.4 121.8 reduce-scatter.19
  894.3 68.5 all-gather.22
  1097.6 121.8 reduce-scatter.23
  1223.1 57.3 reduce-scatter.35
  1284.9 54.3 reduce-scatter.33
  1343.3 168.9 all-reduce.3
  1515.7 55.1 reduce-scatter.31
  1575.4 103.6 reduce-scatter.27
  1683.5 104.3 reduce-scatter.29
  1792.3 61.2 reduce-scatter.25
where the time goes:
time: 1870 us; the launch traced here: 1860 us
  waiting for transfers between devices  1220 us (65%)
  matrix products  305 us (16%)
  other arithmetic  160 us (9%)
  local copies, waits for them, and re-layouts  80.6 us (4%)
  blocking collectives  74.8 us (4%)
    unnamed x23, waiting for transfers between devices  265 us
    reduce_scatter x1, waiting for transfers between devices, on_device(): lax.psum_scatter(jnp.einsum('sbc,cd->sbd', row_block, out_full, preferred...  121 us
    reduce_scatter x1, waiting for transfers between devices, on_device(): lax.psum_scatter(jnp.einsum('sbf,fd->sbd', row_block, down_full, preferre...  113 us
    reduce_scatter x1, waiting for transfers between devices, on_device(): lax.psum_scatter(down_weight_grad, 'dp', scatter_dimension=1, tiled=True)  109 us
    reduce_scatter x1, waiting for transfers between devices, on_device(): lax.psum_scatter(up_weight_grad, 'dp', scatter_dimension=0, tiled=True)  104 us
    reduce_scatter x1, waiting for transfers between devices, on_device(): lax.psum_scatter(jnp.einsum('sbf,df->sbd', row_block, up_back, preferred_...  103 us
    reduce_scatter x1, waiting for transfers between devices, on_device(): lax.psum_scatter(jnp.einsum('sbc,dc->sbd', row_block, qkv_back, preferred...  89.7 us
    all_gather x1, waiting for transfers between devices, on_device(): normed_all_two = lax.all_gather(normed_two, 'tensor', axis=0, tiled=True)  68.5 us
  transfers between devices with their start and end apart: 19, of which 15 were waited for; matrix products, arithmetic and copies ran while one was open for 18% of the time, Pallas kernels for 0%

commit v1 on v0

--- a/solution.py
+++ b/solution.py
@@ -2,10 +2,34 @@
 import jax.numpy as jnp
 from jax import lax
 from jax.sharding import PartitionSpec as P
+from jax.lax import axis_index, axis_size, ppermute
 
 HD = 64
 epsilon = 1e-06
 masked_score = -1e30
+
+
+def register_thing_for(body, dim_at):
+    carry = list(body.shape[1:])
+    carry[dim_at] *= body.shape[0]
+    return jnp.moveaxis(body, 0, dim_at).reshape(carry)
+
+
+def finish_strips_all(z, mesh_dim):
+    upper, block_now = (axis_size(mesh_dim), axis_index(mesh_dim))
+    formed, current_value = (z[None], 1)
+    while current_value < upper:
+        carry_in = ppermute(
+            formed,
+            axis_name=mesh_dim,
+            perm=[(dev_i, dev_i ^ current_value) for dev_i in range(upper)],
+        )
+        arr_next = block_now & current_value == 0
+        formed = jnp.concatenate(
+            [jnp.where(arr_next, formed, carry_in), jnp.where(arr_next, carry_in, formed)]
+        )
+        current_value *= 2
+    return formed
 
 
 def layer_norm(values, gain, shift):
@@ -131,7 +155,7 @@
     )[:, :, None]
     input_float = inputs.astype(jnp.float32)
     normed_one = layer_norm(input_float, gain_one, shift_one).astype(jnp.bfloat16)
-    normed_all = lax.all_gather(normed_one, "tensor", axis=0, tiled=True)
+    normed_all = register_thing_for(finish_strips_all(normed_one, "tensor"), 0)
     qkv_rows = (
         jnp.einsum("sbd,dc->sbc", normed_all, qkv_matrix, preferred_element_type=jnp.float32)
         + bias_row

time: 1870 us -> 1770 us (0.947)
  waiting for transfers between devices: 1220 us -> 1130 us
    unnamed x23 -> x21, waiting for transfers between devices: 265 us -> 79.3 us
    reduce_scatter x0 -> x1, waiting for transfers between devices: none -> 88.6 us  [on_device(): lax.psum_scatter(qkv_weight_grad, 'dp', scatter_dimension=0, tiled=True)]
    all_gather x1 -> x0, waiting for transfers between devices: 54.6 us -> none  [on_device(): normed_all = lax.all_gather(normed_one, 'tensor', axis=0, tiled=True)]
    ppermute x0 -> x1, waiting for transfers between devices: none -> 35.7 us  [finish_strips_all(): ppermute(formed, axis_name=mesh_dim, perm=[(dev_i, dev_i ^ current_value)...]
    reduce_scatter x1, waiting for transfers between devices: 89.7 us -> 113 us  [on_device(): lax.psum_scatter(jnp.einsum('sbc,dc->sbd', row_block, qkv_back, preferred...]
    unnamed x97 -> x92, local copies, waits for them, and re-layouts: 42 us -> 38.3 us
  transfers between devices with their start and end apart: 19 -> 19, of which waited for: 15 -> 15; matrix products, arithmetic and copies ran while one was open for 18% -> 19% of each run, Pallas kernels for 0% -> 0%
where the time goes in v1:
time: 1770 us
  waiting for transfers between devices  1130 us (64%)
  matrix products  308 us (17%)
  other arithmetic  164 us (9%)
  blocking collectives  74.9 us (4%)
  local copies, waits for them, and re-layouts  70.4 us (4%)
    reduce_scatter x1, waiting for transfers between devices, on_device(): lax.psum_scatter(jnp.einsum('sbc,cd->sbd', row_block, out_full, preferred...  119 us
    reduce_scatter x1, waiting for transfers between devices, on_device(): lax.psum_scatter(jnp.einsum('sbf,fd->sbd', row_block, down_full, preferre...  113 us
    reduce_scatter x1, waiting for transfers between devices, on_device(): lax.psum_scatter(jnp.einsum('sbc,dc->sbd', row_block, qkv_back, preferred...  113 us
    reduce_scatter x1, waiting for transfers between devices, on_device(): lax.psum_scatter(down_weight_grad, 'dp', scatter_dimension=1, tiled=True)  109 us
    reduce_scatter x1, waiting for transfers between devices, on_device(): lax.psum_scatter(up_weight_grad, 'dp', scatter_dimension=0, tiled=True)  104 us
    reduce_scatter x1, waiting for transfers between devices, on_device(): lax.psum_scatter(jnp.einsum('sbf,df->sbd', row_block, up_back, preferred_...  103 us
    reduce_scatter x1, waiting for transfers between devices, on_device(): lax.psum_scatter(qkv_weight_grad, 'dp', scatter_dimension=0, tiled=True)  88.6 us
    unnamed x21, waiting for transfers between devices  79.3 us
  transfers between devices with their start and end apart: 19, of which 15 were waited for; matrix products, arithmetic and copies ran while one was open for 19% of the time, Pallas kernels for 0%

profile of v1, /device:TPU:0, one launch (start us, length us, event | category | flops | bytes accessed | tf_op | source)
XLA Modules:
  0.0 1765.3 jit_solution(10803852053678043916)
XLA Ops:
  12.1 23.8 %all_gather.33 = bf16[6,1,512]{0,1,2:T(2,128)(2,1)S(1)} all-gather(bf16[6,1,32]{0,1,2:T(2,128)(2,1)S(1)} %copy.88), channel_id=1, replica_groups=mesh['dp'=16,'tensor'=2] {'dp'}, dimensions={2}, use_global_device_ids=true | all-gather | bytes 6528 | tf_op jit(solution)/shard_map/all_gather | solution.py:129
  50.3 18.3 %all_gather.36 = bf16[2,1,512]{1,0,2:T(2,128)(2,1)S(1)} all-gather(bf16[2,1,32]{1,0,2:T(2,128)(2,1)S(1)} %copy.93), channel_id=1, replica_groups=mesh['dp'=16,'tensor'=2] {'dp'}, dimensions={2}, use_global_device_ids=true | all-gather | bytes 2176 | tf_op jit(solution)/shard_map/all_gather | solution.py:127
  70.9 35.7 %collective-permute-done = bf16[1,320,4,1024]{3,1,2,0:T(8,128)(2,1)} collective-permute-done((bf16[1,320,4,1024]{3,1,2,0:T(8,128)(2,1)}, bf16[1,320,4,1024]{3,1,2,0:T(8,128)(2,1)}, u32[]{:S(2)}, u32[]{:S(2)}) %collective-permute-start) | collective-permute-done | bytes 2621472 | tf_op jit(solution)/shard_map/ppermute | solution.py:22
  117.1 14.0 fusion.50
  131.2 10.6 copy.94
  147.1 51.8 %while.22 = (s32[]{:T(128)}, bf16[4,640,8,64]{1,3,2,0:T(8,128)(2,1)}, f32[4,8,640]{2,1,0:T(8,128)}, bf16[4,640,8,64]{1,3,2,0:T(8,128)(2,1)}, pred[4,640]{1,0:T(4...) while((s32[]{:T(128)}, ...), condition=%wide.region_5.6_spmd, body=%wide.region_2.5_spmd.sunk | while | flops 878504960 | bytes 42113112 | solution.py:168
  203.8 8.9 fusion.79
  213.5 118.7 %reduce-scatter.19.cloned.1.call-done = f32[320,4,1024]{2,0,1:T(8,128)} async-done(((f32[640,4,1024]{2,0,1:T(8,128)}), f32[320,4,1024]{2,0,1:T(8,128)}) %reduce-scatter.19.cloned.1.call-update) | async-done | bytes 5242896 | tf_op jit(solution)/shard_map/reduce_scatter | solution.py:171
  341.0 7.3 fusion.75
  349.2 21.3 %all_gather.40 = bf16[1,2048]{1,0:T(2,128)(2,1)S(1)} all-gather(bf16[1,128]{1,0:T(2,128)(2,1)S(1)} %copy-done.29), channel_id=1, replica_groups=mesh['dp'=16,'tensor'=2] {'dp'}, dimensions={1}, use_global_device_ids=true | all-gather | bytes 4352 | tf_op jit(solution)/shard_map/all_gather | solution.py:128
  370.5 14.3 all-gather.14.cloned.1.call-done
  384.9 68.5 %all-gather.12.cloned.1.call-done = bf16[640,4,1024]{2,0,1:T(8,128)(2,1)} async-done(((bf16[320,4,1024]{2,0,1:T(8,128)(2,1)}), bf16[640,4,1024]{2,0,1:T(8,128)(2,1)}) %all-gather.12.cloned.1.call-update) | async-done | bytes 5242896 | tf_op jit(solution)/shard_map/all_gather | solution.py:179
  453.4 24.9 %fusion.66 = (u8[640,2048]{1,0:T(8,128)(4,1)S(1)}, u8[640,2048]{1,0:T(8,128)(4,1)S(1)}, f32[640,4,2048]{2,0,1:T(8,128)}) fusion(f32[2048]{0:T(1024)S(1)} %bitcast.244, bf16[640,4,1024]{2,0,1:T(8,128)(2,1)} %all-gather.12.cloned.1.call-done, bf16[1024,2048]{1,0:T(8,128)(2,1)} %all-gather.14.cloned.1.call-done), kind=kOutput, calls=%fused_computation.109 | convolution fusion | flops 10808197120 | bytes 33038336 | tf_op jit(solution)/shard_map/sbd,df->sbf/dot_general | solution.py:181
  478.2 51.1 %multiply_convert_fusion.1 = (bf16[640,4,2048]{2,0,1:T(8,128)(2,1)}, f32[640,4,2048]{2,0,1:T(8,128)}) fusion(f32[640,4,2048]{2,0,1:T(8,128)} %get-tuple-element.226, f32[2048]{0:T(1024)S(1)} %bitcast.245, u8[640,2048]{1,0:T(8,128)(4,1)S(1)} %get-tuple-element.154, u8[640,2048]{1,0:T(8,128)(4,1)S(1)} %get-tuple-element.153), kind=kLoop, calls=%fused_computation.64 | loop fusion | flops 372244480 | bytes 55058432 | tf_op jit(solution)/shard_map/convert_element_type | solution.py:184
  529.4 46.7 %all-gather.16.cloned.1.call-done = bf16[2048,1024]{0,1:T(8,128)(2,1)} async-done(((bf16[2048,64]{0,1:T(8,128)(2,1)}), bf16[2048,1024]{0,1:T(8,128)(2,1)}) %all-gather.16.cloned.1.call-update) | async-done | bytes 4194320 | tf_op jit(solution)/shard_map/all_gather | solution.py:126
  576.1 28.4 %convert_reduce_fusion = (f32[2048]{0:T(1024)}, bf16[640,4,2048]{2,0,1:T(8,128)(2,1)}) fusion(f32[640,4,2048]{2,0,1:T(8,128)} %get-tuple-element.198, bf16[640,4,1024]{2,0,1:T(8,128)(2,1)} %all-gather.18.cloned.1.call-done, bf16[2048,1024]{0,1:T(8,128)(2,1)} %all-gather.16.cloned.1.call-done, f32[640,4,2048]{2,0,1:T(8,128)} %get-tuple-element.226, ...), kind=kOutput, calls=%fused_computation.62 | convolution fusion | flops 10826545152 | bytes 61882368 | tf_op jit(solution)/shard_map/sbd,fd->sbf/dot_general | solution.py:201
  604.6 17.4 fusion.70
  622.0 17.5 fusion.68
  639.6 102.9 %reduce-scatter.23.cloned.1.call-done = f32[320,4,1024]{2,0,1:T(8,128)} async-done(((f32[640,4,1024]{2,0,1:T(8,128)}), f32[320,4,1024]{2,0,1:T(8,128)}) %reduce-scatter.23.cloned.1.call-update) | async-done | bytes 5242896 | tf_op jit(solution)/shard_map/reduce_scatter | solution.py:209
  742.5 6.0 fusion.92
  753.2 113.4 %reduce-scatter.21.cloned.1.call-done = f32[320,4,1024]{2,0,1:T(8,128)} async-done(((f32[640,4,1024]{2,0,1:T(8,128)}), f32[320,4,1024]{2,0,1:T(8,128)}) %reduce-scatter.21.cloned.1.call-update) | async-done | bytes 5242896 | tf_op jit(solution)/shard_map/reduce_scatter | solution.py:186
  866.7 11.6 fusion.94
  882.8 68.5 %all-gather.20.cloned.1.call-done = bf16[640,4,1024]{2,0,1:T(8,128)(2,1)} async-done(((bf16[320,4,1024]{2,0,1:T(8,128)(2,1)}), bf16[640,4,1024]{2,0,1:T(8,128)(2,1)}) %all-gather.20.cloned.1.call-update) | async-done | bytes 5242896 | tf_op jit(solution)/shard_map/all_gather | solution.py:220
  951.2 7.2 convolution_convert_fusion
  958.4 113.2 %while.23 = (s32[]{:T(128)}, bf16[4,640,1536]{1,2,0:T(8,128)(2,1)}, bf16[4,640,8,64]{1,3,2,0:T(8,128)(2,1)S(1)}, pred[4,640]{1,0:T(4,128)(4,1)S(1)}, bf16[4,640,...) while((s32[]{:T(128)}, bf16[4,640,1536]{1,2,0:T(8,128)(2,1)}, ...), condition=%wide.region_15.16_spmd, body=%wide.region_13.15_spmd.sunk | while | flops 2134174720 | bytes 108898144 | solution.py:231
  963.7 7.9 multiply_reduce_fusion.5
  971.6 5.9 multiply_convert_fusion.3
  992.0 7.9 multiply_reduce_fusion.5
  999.8 5.9 multiply_convert_fusion.3
  1020.3 7.9 multiply_reduce_fusion.5
  1028.1 5.9 multiply_convert_fusion.3
  1048.6 7.9 multiply_reduce_fusion.5
  1056.4 5.9 multiply_convert_fusion.3
  1071.6 14.4 fusion.51
  1095.0 113.1 %reduce-scatter.25.cloned.1.call-done = f32[320,4,1024]{2,0,1:T(8,128)} async-done(((f32[640,4,1024]{2,0,1:T(8,128)}), f32[320,4,1024]{2,0,1:T(8,128)}) %reduce-scatter.25.cloned.1.call-update) | async-done | bytes 5242896 | tf_op jit(solution)/shard_map/reduce_scatter | solution.py:244
  1216.1 7.1 all-reduce
  1228.9 17.6 convolution_bitcast_fusion.1
  1246.5 17.4 convolution_bitcast_fusion
  1264.2 7.7 fusion.82
  1271.9 14.0 convolution_bitcast_fusion.2
  1287.4 8.3 copy.101
  1295.7 31.6 %reduce-scatter.37.cloned.1.call-done = f32[32,2]{1,0:T(8,128)} async-done(((f32[512,2]{1,0:T(8,128)}), f32[32,2]{1,0:T(8,128)}) %reduce-scatter.37.cloned.1.call-update) | async-done | bytes 272
  1334.3 5.7 copy.102
  1340.0 45.5 %reduce-scatter.35.cloned.1.call-done = f32[32,6]{1,0:T(8,128)} async-done(((f32[512,6]{1,0:T(8,128)}), f32[32,6]{1,0:T(8,128)}) %reduce-scatter.35.cloned.1.call-update) | async-done | bytes 784
  1389.9 104.3 %reduce-scatter.31.cloned.1.call-done = f32[64,2048]{1,0:T(8,128)} async-done(((f32[1024,2048]{1,0:T(8,128)}), f32[64,2048]{1,0:T(8,128)}) %reduce-scatter.31.cloned.1.call-update) | async-done | bytes 524304 | tf_op jit(solution)/shard_map/reduce_scatter | solution.py:268
  1494.2 109.4 %reduce-scatter.33.cloned.1.call-done = f32[2048,64]{0,1:T(8,128)} async-done(((f32[2048,1024]{0,1:T(8,128)}), f32[2048,64]{0,1:T(8,128)}) %reduce-scatter.33.cloned.1.call-update) | async-done | bytes 524304 | tf_op jit(solution)/shard_map/reduce_scatter | solution.py:269
  1603.6 66.0 %reduce-scatter.29.cloned.1.call-done = f32[512,64]{0,1:T(8,128)} async-done(((f32[512,1024]{0,1:T(8,128)}), f32[512,64]{0,1:T(8,128)}) %reduce-scatter.29.cloned.1.call-update) | async-done | bytes 131088 | tf_op jit(solution)/shard_map/reduce_scatter | solution.py:267
  1669.5 88.6 %reduce-scatter.27.cloned.1.call-done = f32[64,3,512]{2,0,1:T(8,128)} async-done(((f32[1024,3,512]{2,0,1:T(8,128)}), f32[64,3,512]{2,0,1:T(8,128)}) %reduce-scatter.27.cloned.1.call-update) | async-done | bytes 393232 | tf_op jit(solution)/shard_map/reduce_scatter | solution.py:266
  (230 shorter events, 206.6 us)
Async XLA Ops:
  7.2 36.4 %copy-start.1 = (bf16[320,4,1024]{2,1,0:T(4,128)(2,1)S(1)}, bf16[320,4,1024]{2,1,0:T(4,128)(2,1)}, u32[]{:S(2)}) copy-start(bf16[320,4,1024]{2,1,0:T(4,128)(2,1)} %param.19) | copy-start | bytes 7864324
  7.2 106.7 %all-gather.8.cloned.1.call-start = ((), (), s32[]{:S(2)}) async-start(), calls=%async_computation.11 | async-start | bytes 3342336 | tf_op jit(solution)/shard_map/all_gather | solution.py:123
  7.9 195.9 %all-gather.10.cloned.1.call-start = ((), (), s32[]{:S(2)}) async-start(), calls=%async_computation.12 | async-start | bytes 1114112 | tf_op jit(solution)/shard_map/all_gather | solution.py:124
  40.4 9.9 copy-start.28
  40.4 30.5 %copy-start.26 = (s32[4,640]{1,0:T(4,128)S(1)}, s32[4,640]{1,0:T(4,128)}, u32[]{:S(2)}) copy-start(s32[4,640]{1,0:T(4,128)} %param.20) | copy-start | bytes 30724
  43.6 66.5 %copy-start.10 = (f32[320,4]{0,1:T(4,128)}, f32[320,4]{0,1:T(4,128)S(1)}, u32[]{:S(2)}) copy-start(f32[320,4]{0,1:T(4,128)S(1)} %broadcast_multiply_fusion.1) | copy-start | bytes 15364
  45.2 64.9 %copy-start.12 = (f32[320,4]{0,1:T(4,128)}, f32[320,4]{0,1:T(4,128)S(1)}, u32[]{:S(2)}) copy-start(f32[320,4]{0,1:T(4,128)S(1)} %fusion.90) | copy-start | bytes 15364
  45.8 64.3 %copy-start.14 = (f32[1,2,512]{2,0,1:T(1,128)}, f32[1,2,512]{2,0,1:T(1,128)S(1)}, u32[]{:S(2)}) copy-start(f32[1,2,512]{2,0,1:T(1,128)S(1)} %get-tuple-element.222) | copy-start | bytes 12292
  48.2 58.4 %collective-permute-start = (bf16[1,320,4,1024]{3,1,2,0:T(8,128)(2,1)}, bf16[1,320,4,1024]{3,1,2,0:T(8,128)(2,1)}, u32[]{:S(2)}, u32[]{:S(2)}) collective-permute-start(bf16[1,320,4,1024]{3,1,2,0:T(8,128)(2,1)} %fusion.76), channel_id=1, source_target_pairs={{0,1},{1,0},{2,3},{3,2},{4,5},{5,4},{6,7},{7,6},{8,9},{9,8},{10,11... | collective-permute-start | bytes 7864328 | tf_op jit(solution)/shard_map/ppermute | solution.py:22
  50.1 282.1 %reduce-scatter.19.cloned.1.call-start = ((), (), s32[]{:S(2)}) async-start(), calls=%async_computation.13 | async-start | bytes 15728640 | tf_op jit(solution)/shard_map/reduce_scatter | solution.py:171
  117.1 14.0 copy-start.9
  198.8 13.9 copy-start.7
  212.7 119.6 %copy-start.2 = (bf16[320,4,1024]{2,1,0:T(4,128)(2,1)S(1)}, bf16[320,4,1024]{2,1,0:T(4,128)(2,1)}, u32[]{:S(2)}) copy-start(bf16[320,4,1024]{2,1,0:T(4,128)(2,1)} %param.19) | copy-start | bytes 7864324
  212.7 119.6 %copy-start.22 = (f32[1,2,512]{2,0,1:T(1,128)S(1)}, f32[1,2,512]{2,0,1:T(1,128)}, u32[]{:S(2)}) copy-start(f32[1,2,512]{2,0,1:T(1,128)} %get-tuple-element.221) | copy-start | bytes 12292
  212.7 172.1 %all-gather.14.cloned.1.call-start = ((), (), s32[]{:S(2)}) async-start(), calls=%async_computation.15 | async-start | bytes 4456448 | tf_op jit(solution)/shard_map/all_gather | solution.py:125
  213.3 240.1 %all-gather.12.cloned.1.call-start = ((), (), s32[]{:S(2)}) async-start(), calls=%async_computation.14 | async-start | bytes 7864320 | tf_op jit(solution)/shard_map/all_gather | solution.py:179
  336.4 2.4 copy-start
  336.4 2.4 copy-start.16
  336.4 2.3 copy-start.19
  340.9 188.5 %all-gather.18.cloned.1.call-start = ((), (), s32[]{:S(2)}) async-start(), calls=%async_computation.18 | async-start | bytes 7864320 | tf_op jit(solution)/shard_map/all_gather | solution.py:197
  341.0 8.2 copy-start.29
  348.4 227.7 %all-gather.16.cloned.1.call-start = ((), (), s32[]{:S(2)}) async-start(), calls=%async_computation.16 | async-start | bytes 4456448 | tf_op jit(solution)/shard_map/all_gather | solution.py:126
  349.1 393.3 %reduce-scatter.23.cloned.1.call-start = ((), (), s32[]{:S(2)}) async-start(), calls=%async_computation.19 | async-start | bytes 15728640 | tf_op jit(solution)/shard_map/reduce_scatter | solution.py:209
  622.0 244.7 %reduce-scatter.21.cloned.1.call-start = ((), (), s32[]{:S(2)}) async-start(), calls=%async_computation.17 | async-start | bytes 15728640 | tf_op jit(solution)/shard_map/reduce_scatter | solution.py:186
  639.5 311.7 %all-gather.20.cloned.1.call-start = ((), (), s32[]{:S(2)}) async-start(), calls=%async_computation.20 | async-start | bytes 7864320 | tf_op jit(solution)/shard_map/all_gather | solution.py:220
  742.5 6.0 copy-start.4
  748.5 118.2 %copy-start.21 = (f32[1,2,512]{2,0,1:T(1,128)S(1)}, f32[1,2,512]{2,0,1:T(1,128)}, u32[]{:S(2)}) copy-start(f32[1,2,512]{2,0,1:T(1,128)} %get-tuple-element.218) | copy-start | bytes 12292
  878.3 2.3 copy-start.6
  882.5 325.6 %reduce-scatter.25.cloned.1.call-start = ((), (), s32[]{:S(2)}) async-start(), calls=%async_computation.21 | async-start | bytes 15728640 | tf_op jit(solution)/shard_map/reduce_scatter | solution.py:244
  882.8 75.7 %copy-start.8 = (bf16[4,640,8,64]{1,3,2,0:T(8,128)(2,1)S(1)}, bf16[4,640,8,64]{1,3,2,0:T(8,128)(2,1)}, u32[]{:S(2)}) copy-start(bf16[4,640,8,64]{1,3,2,0:T(8,128)(2,1)} %copy-done.7) | copy-start | bytes 7864324
  1086.0 1.2 copy-start.27
  1086.0 2.7 copy-start.25
  1086.0 2.7 copy-start.20
  1086.0 2.7 copy-start.23
  1086.0 2.7 copy-start.24
  1086.1 199.9 %reduce-scatter.39.cloned.1.call-start = ((), (), s32[]{:S(2)}) async-start(), calls=%async_computation.28 | async-start | bytes 1114112
  1088.6 119.5 %copy-start.3 = (bf16[320,4,1024]{2,1,0:T(4,128)(2,1)S(1)}, bf16[320,4,1024]{2,1,0:T(4,128)(2,1)}, u32[]{:S(2)}) copy-start(bf16[320,4,1024]{2,1,0:T(4,128)(2,1)} %param.19) | copy-start | bytes 7864324
  1088.6 119.5 %copy-start.11 = (f32[320,4]{0,1:T(4,128)S(1)}, f32[320,4]{0,1:T(4,128)}, u32[]{:S(2)}) copy-start(f32[320,4]{0,1:T(4,128)} %copy-done.10) | copy-start | bytes 15364
  1088.6 119.5 %copy-start.15 = (f32[1,2,512]{2,0,1:T(1,128)S(1)}, f32[1,2,512]{2,0,1:T(1,128)}, u32[]{:S(2)}) copy-start(f32[1,2,512]{2,0,1:T(1,128)} %copy-done.14) | copy-start | bytes 12292
  1088.6 238.7 %reduce-scatter.37.cloned.1.call-start = ((), (), s32[]{:S(2)}) async-start(), calls=%async_computation.27 | async-start | bytes 278528
  1093.3 119.1 %copy-start.18 = (f32[320,4]{0,1:T(4,128)S(1)}, f32[320,4]{0,1:T(4,128)}, u32[]{:S(2)}) copy-start(f32[320,4]{0,1:T(4,128)} %copy-done.17) | copy-start | bytes 15364
  1093.3 119.2 %copy-start.13 = (f32[320,4]{0,1:T(4,128)S(1)}, f32[320,4]{0,1:T(4,128)}, u32[]{:S(2)}) copy-start(f32[320,4]{0,1:T(4,128)} %copy-done.12) | copy-start | bytes 15364
  1095.0 290.5 %reduce-scatter.35.cloned.1.call-start = ((), (), s32[]{:S(2)}) async-start(), calls=%async_computation.26 | async-start | bytes 278528
  1208.1 4.4 copy-start.5
  1228.8 265.4 %reduce-scatter.31.cloned.1.call-start = ((), (), s32[]{:S(2)}) async-start(), calls=%async_computation.24 | async-start | bytes 8912896 | tf_op jit(solution)/shard_map/reduce_scatter | solution.py:268
  1246.4 357.1 %reduce-scatter.33.cloned.1.call-start = ((), (), s32[]{:S(2)}) async-start(), calls=%async_computation.25 | async-start | bytes 8912896 | tf_op jit(solution)/shard_map/reduce_scatter | solution.py:269
  1263.9 405.7 %reduce-scatter.29.cloned.1.call-start = ((), (), s32[]{:S(2)}) async-start(), calls=%async_computation.23 | async-start | bytes 2228224 | tf_op jit(solution)/shard_map/reduce_scatter | solution.py:267
  1271.9 486.2 %reduce-scatter.27.cloned.1.call-start = ((), (), s32[]{:S(2)}) async-start(), calls=%async_computation.22 | async-start | bytes 6684672 | tf_op jit(solution)/shard_map/reduce_scatter | solution.py:266
  (2 other events, 1.3 us)
Sparse Core Ops, SparseCore 0:
  10.2 49.1 all-gather.7
  61.6 36.5 all-gather.9
  212.9 119.3 reduce-scatter.18
  334.3 50.5 all-gather.13
  386.3 67.0 all-gather.11
  454.8 68.5 all-gather.17
  525.5 50.5 all-gather.15
  622.1 120.3 reduce-scatter.22
  744.8 121.8 reduce-scatter.20
  882.6 68.5 all-gather.19
  1086.2 121.8 reduce-scatter.24
  1211.6 57.4 reduce-scatter.38
  1273.0 54.2 reduce-scatter.36
  1331.1 54.3 reduce-scatter.34
  1390.5 103.5 reduce-scatter.30
  1499.2 104.3 reduce-scatter.32
  1608.2 61.3 reduce-scatter.28
  1673.9 84.1 reduce-scatter.26
